TPU v7x, 768 devices: a whole 4x8x12 slice. The times are simulated.
768 devices in a mesh: dom: 64 (over y, z_lo, core), feat: 12 (over z_hi, x).
Axes of the slice: x: 4, y: 8, z: 12 (z_hi: 3, z_lo: 4; z = z_hi * 4 + z_lo), core: 2. Of those that a mesh axis runs over, the one named last changes fastest.
Arguments:
- node_state: bfloat16 [1179648, 128], P(('dom', 'feat')), may hold values from -6 to 6
- w_msg: bfloat16 [128, 128], replicated, may hold values from -0.5 to 0.5
- w_first: bfloat16 [256, 128], replicated, may hold values from -0.375 to 0.375
- b_first: float32 [128], replicated, may hold values from -3 to 3
- w_second: bfloat16 [128, 128], replicated, may hold values from -0.5 to 0.5
- b_second: float32 [128], replicated, may hold values from -3 to 3
- ln_gain: float32 [128], replicated, may hold values from 0.5 to 1.5
- col_index: int32 [9216, 4], P(('dom', 'feat')), may hold values from 0 to 9215, as said below
- edge_counts: int32 [9216, 4, 128, 128], P(('dom', 'feat')), may hold values from 0 to 3, as said below
- cotangent: bfloat16 [1179648, 128], P(('dom', 'feat')), may hold values from -14 to 14
Outputs:
- updated: bfloat16 [1179648, 128], P(('dom', 'feat'))
- grad_state: bfloat16 [1179648, 128], P(('dom', 'feat'))
- grad_w_msg: float32 [128, 128], replicated
- grad_w_first: float32 [256, 128], replicated
- grad_b_first: float32 [128], replicated
- grad_w_second: float32 [128, 128], replicated
- grad_b_second: float32 [128], replicated
- grad_gain: float32 [128], replicated
Inputs may be any that keep to these rules, and one draw needn't show every extreme that they name: `col_index`: tile 0 of block row b is block b itself; every other tile's column lies within 2 blocks of b, reflected at the two ends of the curve; columns of one block row may repeat. `edge_counts`: most entries are zero.
All inputs are finite; a program needn't handle non-finite values.
Results may differ from a plain program's by a relative error of at most 0.0093.
Values may be sent and summed in bfloat16 or wider, within the bound.
A program may use at most 32 MiB of HBM per device.

v0:
```python
import math

import jax
import jax.numpy as jnp
from jax import lax
from jax.sharding import PartitionSpec as P

WIN = 2


epsilon = 1e-05


def with_halo(cells, sides, width):
    for axis, dim in sides:
        count = lax.axis_size(axis)
        ends = count - 1
        head = lax.slice_in_dim(cells, 0, width, axis=dim)
        tail = lax.slice_in_dim(cells, cells.shape[dim] - width, cells.shape[dim], axis=dim)
        cells = jnp.concatenate(
            [
                lax.ppermute(tail, axis, [(i, (i + 1) % count) for i in range(ends)]),
                cells,
                lax.ppermute(head, axis, [((i + 1) % count, i) for i in range(ends)]),
            ],
            axis=dim,
        )
    return cells


def passed_along(block, axis, distance):
    devices = range(lax.axis_size(axis))
    route = [(i - distance, i) for i in devices if i - distance in devices]
    return lax.ppermute(block, axis, route)


def inner_rows(left, right):
    return lax.dot_general(
        left, right, (((0,), (0,)), ((), ())), preferred_element_type=jnp.float32
    )


def times_transposed(left, right):
    return lax.dot_general(
        left, right, (((1,), (1,)), ((), ())), preferred_element_type=jnp.float32
    )


def shards(
    node_state,
    w_msg,
    w_first,
    b_first,
    w_second,
    b_second,
    ln_gain,
    col_index,
    edge_counts,
    cotangent,
):
    node_rows, features = node_state.shape
    block_count, tile_count, block_size, _ = edge_counts.shape
    span_blocks = WIN
    devices = lax.axis_size("dom") * lax.axis_size("feat")
    grad_scale = 1.0 / math.sqrt(node_rows * devices)
    messages = jnp.dot(node_state, w_msg, preferred_element_type=jnp.float32).astype(jnp.bfloat16)
    extended = with_halo(messages, ((("dom", "feat"), 0),), span_blocks * block_size)
    ext_blocks = extended.reshape(block_count + 2 * span_blocks, block_size, features)
    first_block = lax.axis_index(("dom", "feat")) * block_count
    local_col = col_index - first_block + span_blocks
    gathered = ext_blocks[local_col]
    tile_weights = edge_counts.astype(jnp.bfloat16)
    aggregate = jnp.einsum(
        "btij,btjh->bih", tile_weights, gathered, preferred_element_type=jnp.float32
    )
    aggregate = aggregate.reshape(node_rows, features).astype(jnp.bfloat16)
    joined = jnp.concatenate([node_state, aggregate], axis=1)
    pre_hidden = jnp.dot(joined, w_first, preferred_element_type=jnp.float32) + b_first
    activated = jax.nn.silu(pre_hidden).astype(jnp.bfloat16)
    pre_norm = jnp.dot(activated, w_second, preferred_element_type=jnp.float32) + b_second
    row_mean = jnp.mean(pre_norm, axis=-1, keepdims=True)
    centred = pre_norm - row_mean
    inv_std = lax.rsqrt(jnp.mean(centred * centred, axis=-1, keepdims=True) + epsilon)
    normed = centred * inv_std
    updated = (node_state.astype(jnp.float32) + ln_gain * normed).astype(jnp.bfloat16)
    cot_f32 = cotangent.astype(jnp.float32)
    d_normed = cot_f32 * ln_gain
    d_pre_norm = (
        inv_std
        * (
            d_normed
            - jnp.mean(d_normed, axis=-1, keepdims=True)
            - normed * jnp.mean(d_normed * normed, axis=-1, keepdims=True)
        )
    ).astype(jnp.bfloat16)
    sigmoid_z = jax.nn.sigmoid(pre_hidden)
    d_pre_hidden = (
        times_transposed(d_pre_norm, w_second) * sigmoid_z * (1.0 + pre_hidden * (1.0 - sigmoid_z))
    ).astype(jnp.bfloat16)
    d_joined = times_transposed(d_pre_hidden, w_first)
    d_aggregate = (
        d_joined[:, features:].astype(jnp.bfloat16).reshape(block_count, block_size, features)
    )
    contribution = jnp.einsum(
        "btij,bih->btjh", tile_weights, d_aggregate, preferred_element_type=jnp.float32
    )
    slot_ids = jnp.arange(block_count + 2 * span_blocks, dtype=jnp.int32)
    one_hot = (local_col[:, :, None] == slot_ids[None, None, :]).astype(jnp.float32)
    ext_grad = jnp.einsum("btc,btjh->cjh", one_hot, contribution, precision=lax.Precision.HIGHEST)
    lower_part = ext_grad[:span_blocks]
    upper_part = ext_grad[block_count + span_blocks :]
    own_part = ext_grad[span_blocks : block_count + span_blocks]
    from_below = passed_along(upper_part.astype(jnp.bfloat16), ("dom", "feat"), 1).astype(
        upper_part.dtype
    )
    from_above = passed_along(lower_part.astype(jnp.bfloat16), ("dom", "feat"), -1).astype(
        lower_part.dtype
    )
    summed_grad = own_part.at[:span_blocks].add(from_below)
    summed_grad = summed_grad.at[block_count - span_blocks :].add(from_above)
    d_messages = summed_grad.reshape(node_rows, features).astype(jnp.bfloat16)
    grad_state = (cot_f32 + d_joined[:, :features] + times_transposed(d_messages, w_msg)).astype(
        jnp.bfloat16
    )
    terms = (
        inner_rows(node_state, d_messages) * grad_scale,
        inner_rows(joined, d_pre_hidden) * grad_scale,
        jnp.sum(d_pre_hidden, axis=0, dtype=jnp.float32) * grad_scale,
        inner_rows(activated, d_pre_norm) * grad_scale,
        jnp.sum(d_pre_norm, axis=0, dtype=jnp.float32) * grad_scale,
        jnp.sum(cot_f32 * normed, axis=0) * grad_scale,
    )
    totals = lax.psum((terms[0], terms[1], terms[2], terms[3], terms[4], terms[5]), ("dom", "feat"))
    return (updated, grad_state, totals[0], totals[1], totals[2], totals[3], totals[4], totals[5])


def solution(mesh):
    return jax.shard_map(
        shards,
        mesh=mesh,
        in_specs=(
            P(("dom", "feat"), None),
            P(),
            P(),
            P(),
            P(),
            P(),
            P(),
            P(("dom", "feat"), None),
            P(("dom", "feat"), None, None, None),
            P(("dom", "feat"), None),
        ),
        out_specs=(
            P(("dom", "feat"), None),
            P(("dom", "feat"), None),
            P(),
            P(),
            P(),
            P(),
            P(),
            P(),
        ),
        check_vma=False,
    )
```

profile of v0, /device:TPU:1, one launch (start us, length us, event | category | flops | bytes accessed | tf_op | source)
XLA Modules:
  0.0 666.6 jit_solution(8073881219025596406)
XLA Ops:
  7.2 0.0 all-reduce.4.cloned.1.call-start
  7.2 1.3 convolution_convert_fusion
  8.6 3.9 collective-permute-start
  12.5 15.8 %collective-permute-start.1 = (bf16[256,128]{1,0:T(8,128)(2,1)S(1)}, bf16[256,128]{1,0:T(8,128)(2,1)S(1)}, u32[]{:S(2)}, u32[]{:S(2)}) collective-permute-start(bf16[256,128]{1,0:T(8,128)(2,1)S(1)} %get-tuple-element.71), channel_id=1, source_target_pairs={{1,0},{2,1},{3,2},{4,3},{5,4},{6,5},{7,6},{8,7},{9,8},{10,9},{11,1... | collective-permute-start | bytes 196616 | tf_op jit(solution)/shard_map/ppermute | solution.py:24
  28.4 1.9 copy.35
  30.3 0.1 copy.36
  30.4 0.1 reshape.114
  30.5 0.9 copy.37
  31.4 0.8 pad_maximum_fusion.1
  32.3 3.1 gather_fusion
  35.4 2.0 fusion.3
  37.5 0.4 multiply_convert_fusion
  37.9 0.3 copy-done.12
  38.2 0.3 fusion.25
  38.6 0.1 multiply_reduce_fusion
  38.7 0.2 copy-done.3
  38.9 0.4 fusion.12
  39.3 1.2 convert_reduce_fusion
  40.4 0.9 convolution_multiply_fusion.2
  41.4 0.5 convert_reduce_fusion.1
  41.8 1.1 convolution_multiply_fusion.1
  42.9 0.4 fusion.26
  43.3 0.1 slice.100
  43.4 1.1 copy-done.5
  44.4 0.6 convolution_bitcast_fusion
  45.1 3.5 copy.40
  48.5 4.3 convolution_bitcast_fusion.1
  52.9 0.3 copy.56
  53.2 0.7 fusion.23
  53.9 1.9 collective-permute-start.2
  55.8 0.3 copy.41
  56.2 0.6 copy-done.9
  56.8 0.9 copy.45
  57.7 0.3 copy.54
  58.0 9.8 %collective-permute-start.3 = (bf16[2,128,128]{2,1,0:T(8,128)(2,1)}, bf16[2,128,128]{2,1,0:T(8,128)(2,1)}, u32[]{:S(2)}, u32[]{:S(2)}) collective-permute-start(bf16[2,128,128]{2,1,0:T(8,128)(2,1)} %get-tuple-element.68), channel_id=1, source_target_pairs={{1,0},{2,1},{3,2},{4,3},{5,4},{6,5},{7,6},{8,7},{9,8},{10,9},{11,1... | collective-permute-start | bytes 196616 | tf_op jit(solution)/shard_map/ppermute | solution.py:34
  67.8 0.1 slice.88
  67.9 111.0 %all-reduce = (f32[128]{0:T(128)}, f32[128]{0:T(128)}, f32[128]{0:T(128)}) all-reduce(f32[128]{0:T(128)S(1)} %broadcast_multiply_fusion.5, f32[128]{0:T(128)S(1)} %broadcast_multiply_fusion.4, f32[128]{0:T(128)S(1)} %broadcast_multiply_fusion.3), channel_id=1, replica_groups=mesh['dom'=64,'feat'=12] {'dom','feat'}, use_global_device_ids=true, to_apply=%region_7.8 | all-reduce | flops 384 | bytes 3072 | tf_op jit(solution)/shard_map/psum | solution.py:133
  178.9 0.9 fusion.16
  179.7 0.9 fusion.15
  180.6 0.1 convert_element_type.71
  180.7 0.9 fusion.4
  181.6 0.0 all-reduce.4.cloned.1.call-update
  181.7 0.3 fusion.2
  181.9 0.9 copy.46
  182.9 472.3 %all-reduce.4.cloned.1.call-done = (f32[128,128]{0,1:T(8,128)}, f32[256,128]{1,0:T(8,128)}, f32[128,128]{1,0:T(8,128)}) async-done(((f32[128,128]{0,1:T(8,128)}, f32[256,128]{1,0:T(8,128)}, f32[128,128]{1,0:T(8,128)}), (f32[128,128]{0,1:T(8,128)}, f32[256,128]{1,0:T(8,128)}, f32[128,128]{1,0:T(8,128)})) %all-reduce.4.cloned.1.call-update) | async-done | bytes 262160 | tf_op jit(solution)/shard_map/psum | solution.py:133
  655.2 1.6 copy.47
  656.8 1.6 copy.62
  658.3 1.5 copy.63
  (45 shorter events, 0.1 us)
Async XLA Ops:
  7.2 30.3 %copy-start = (bf16[256,128]{1,0:T(8,128)(2,1)S(1)}, bf16[256,128]{1,0:T(8,128)(2,1)}, u32[]{:S(2)}) copy-start(bf16[256,128]{1,0:T(8,128)(2,1)} %param.16) | copy-start | bytes 196612
  7.2 23.1 %copy-start.14 = (s32[12,4]{0,1:T(4,128)S(1)}, s32[12,4]{0,1:T(4,128)}, u32[]{:S(2)}) copy-start(s32[12,4]{0,1:T(4,128)} %param.21) | copy-start | bytes 580
  7.2 23.3 %copy-start.10 = (bf16[1536,128]{1,0:T(8,128)(2,1)S(1)}, bf16[1536,128]{1,0:T(8,128)(2,1)}, u32[]{:S(2)}) copy-start(bf16[1536,128]{1,0:T(8,128)(2,1)} %param.23) | copy-start | bytes 1179652
  7.2 648.0 %all-reduce.4.cloned.1.call-start = ((), (), s32[]{:S(2)}) async-start(), calls=%async_computation | async-start | bytes 524288 | tf_op jit(solution)/shard_map/psum | solution.py:133
  8.6 22.8 %collective-permute-start = (bf16[256,128]{1,0:T(8,128)(2,1)S(1)}, bf16[256,128]{1,0:T(8,128)(2,1)S(1)}, u32[]{:S(2)}, u32[]{:S(2)}) collective-permute-start(bf16[256,128]{1,0:T(8,128)(2,1)S(1)} %get-tuple-element.70), channel_id=1, source_target_pairs={{0,1},{1,2},{2,3},{3,4},{4,5},{5,6},{6,7},{7,8},{8,9},{9,10},{10,1... | collective-permute-start | bytes 196616 | tf_op jit(solution)/shard_map/ppermute | solution.py:22
  12.5 18.9 %collective-permute-start.1 = (bf16[256,128]{1,0:T(8,128)(2,1)S(1)}, bf16[256,128]{1,0:T(8,128)(2,1)S(1)}, u32[]{:S(2)}, u32[]{:S(2)}) collective-permute-start(bf16[256,128]{1,0:T(8,128)(2,1)S(1)} %get-tuple-element.71), channel_id=1, source_target_pairs={{1,0},{2,1},{3,2},{4,3},{5,4},{6,5},{7,6},{8,7},{9,8},{10,9},{11,1... | collective-permute-start | bytes 196616 | tf_op jit(solution)/shard_map/ppermute | solution.py:24
  32.3 3.1 copy-start.1
  35.4 2.0 copy-start.6
  35.4 2.0 copy-start.16
  37.5 0.8 copy-start.12
  37.5 0.8 copy-start.15
  37.9 1.0 copy-start.3
  37.9 1.0 copy-start.13
  38.2 1.0 copy-start.8
  41.8 2.6 copy-start.2
  43.3 1.2 copy-start.5
  53.9 125.0 %collective-permute-start.2 = (bf16[2,128,128]{2,1,0:T(8,128)(2,1)}, bf16[2,128,128]{2,1,0:T(8,128)(2,1)}, u32[]{:S(2)}, u32[]{:S(2)}) collective-permute-start(bf16[2,128,128]{2,1,0:T(8,128)(2,1)} %get-tuple-element.69), channel_id=1, source_target_pairs={{0,1},{1,2},{2,3},{3,4},{4,5},{5,6},{6,7},{7,8},{8,9},{9,10},{10,1... | collective-permute-start | bytes 196616 | tf_op jit(solution)/shard_map/ppermute | solution.py:34
  55.8 1.0 copy-start.9
  55.8 1.9 slice-start
  58.0 122.7 %copy-start.7 = (bf16[1536,128]{1,0:T(8,128)(2,1)S(1)}, bf16[1536,128]{1,0:T(8,128)(2,1)}, u32[]{:S(2)}) copy-start(bf16[1536,128]{1,0:T(8,128)(2,1)} %param.14) | copy-start | bytes 1179652
  58.0 121.7 %collective-permute-start.3 = (bf16[2,128,128]{2,1,0:T(8,128)(2,1)}, bf16[2,128,128]{2,1,0:T(8,128)(2,1)}, u32[]{:S(2)}, u32[]{:S(2)}) collective-permute-start(bf16[2,128,128]{2,1,0:T(8,128)(2,1)} %get-tuple-element.68), channel_id=1, source_target_pairs={{1,0},{2,1},{3,2},{4,3},{5,4},{6,5},{7,6},{8,7},{9,8},{10,9},{11,1... | collective-permute-start | bytes 196616 | tf_op jit(solution)/shard_map/ppermute | solution.py:34
  67.9 113.8 %copy-start.4 = (bf16[1536,128]{0,1:T(8,128)(2,1)S(1)}, bf16[1536,128]{0,1:T(8,128)(2,1)}, u32[]{:S(2)}) copy-start(bf16[1536,128]{0,1:T(8,128)(2,1)} %copy.37) | copy-start | bytes 1179652
  67.9 113.8 %copy-start.11 = (bf16[128,128]{1,0:T(8,128)(2,1)S(1)}, bf16[128,128]{1,0:T(8,128)(2,1)}, u32[]{:S(2)}) copy-start(bf16[128,128]{1,0:T(8,128)(2,1)} %param.15) | copy-start | bytes 98308
Sparse Core Ops, SparseCore 0:
  181.8 473.3 all-reduce.3
where the time goes:
time: 667 us
  waiting for transfers between devices  472 us (71%)
  blocking collectives  111 us (17%)
  starting transfers between devices  31.5 us (5%)
  local copies, waits for them, and re-layouts  20.1 us (3%)
  between operations  14.4 us (2%)
  matrix products  13 us (2%)
    psum x1, waiting for transfers between devices, shards(): lax.psum((terms[0], terms[1], terms[2], terms[3], terms[4], terms[5]), ('...  472 us
    psum x1, blocking collectives, shards(): lax.psum((terms[0], terms[1], terms[2], terms[3], terms[4], terms[5]), ('...  111 us
    ppermute x1, starting transfers between devices, with_halo(): lax.ppermute(head, axis, [((i + 1) % count, i) for i in range(ends)])  15.8 us
  transfers between devices with their start and end apart: 5, of which 1 were waited for; matrix products, arithmetic and copies ran while one was open for 1% of the time, Pallas kernels for 0%

commit v1 on v0

v1 whole, which is shorter than its diff:
```python
import functools
import math

import jax
import jax.numpy as jnp
from jax import lax
from jax.experimental import pallas as pl
from jax.experimental.pallas import tpu as pltpu
from jax.sharding import PartitionSpec as P

MESH = pl.DeviceIdType.MESH
WIN = 2
SPAN = 2 * WIN + 1
EPS = 1e-05
NX, NY, NZ, Z_LO, CORES = 4, 8, 12, 4, 2
PIECE = 8
QUARTER = PIECE * NY
HALF = QUARTER * NX
TOTAL = HALF * CORES
GROUP = 2


def dot(a, b):
    return jnp.dot(a, b, preferred_element_type=jnp.float32)


def dot_rt(a, b):
    return lax.dot_general(a, b, (((1,), (1,)), ((), ())), preferred_element_type=jnp.float32)


def dot_lt(a, b):
    return lax.dot_general(a, b, (((0,), (0,)), ((), ())), preferred_element_type=jnp.float32)


def layer_kernel(
    x_hbm, wmsg_hbm, wf_hbm, bf_hbm, ws_hbm, bs_hbm, gain_hbm, col_hbm, cnt_hbm, cot_hbm,
    upd_out, gs_out, tot_out,
    xe, wmsg, wf, bf, ws, bs, gain, col, cnt, cot,
    band, dag, gsp, dme, pay, r1, a1, r2, a2, r3, a3, r4, out, bh_send, bh_recv,
    in_sem, cnt_sem, halo_s, halo_r, c_s, c_r, x_s, x_r, y_s, y_r, z_s, z_r,
    ay_s, ay_r, ax_s, ax_r, ac_s, ac_r, b_s, b_r,
):
    nb = cnt_hbm.shape[0]
    rows = x_hbm.shape[0]
    blk = cnt_hbm.shape[2]
    edge = WIN * blk
    ndom, nfeat = lax.axis_size("dom"), lax.axis_size("feat")
    count = ndom * nfeat
    dom, feat = lax.axis_index("dom"), lax.axis_index("feat")
    core, z_lo, y = lax.rem(dom, CORES), lax.rem(dom // CORES, Z_LO), dom // (CORES * Z_LO)
    x, z_hi = lax.rem(feat, NX), feat // NX
    z = z_hi * Z_LO + z_lo
    rank = dom * nfeat + feat
    first_block = rank * nb

    def by_rank(r):
        return (r // nfeat, lax.rem(r, nfeat))

    nxt = by_rank(lax.rem(rank + 1, count))
    prv = by_rank(lax.rem(rank + count - 1, count))
    mate = (dom + 1 - 2 * core, feat)

    def at_x(k):
        return (dom, z_hi * NX + lax.rem(x + k, NX))

    def at_y(k):
        return ((lax.rem(y + k, NY) * Z_LO + z_lo) * CORES + core, feat)

    def at_z(k):
        other = lax.rem(z + k, NZ)
        return ((y * Z_LO + lax.rem(other, Z_LO)) * CORES + core, (other // Z_LO) * NX + x)

    peers = [prv, nxt]
    peers += [at_z(k) for k in (6, 5, 7, 4, 8, 3, 9, 2, 10, 1, 11)]
    peers += [at_y(k) for k in range(1, NY)]
    peers += [at_x(k) for k in range(1, NX)]
    peers += [mate]
    barrier = pltpu.get_barrier_semaphore()
    for peer in peers:
        pl.semaphore_signal(barrier, inc=1, device_id=peer, device_id_type=MESH)

    loads = [
        pltpu.make_async_copy(src, dst, in_sem.at[i])
        for i, (src, dst) in enumerate(
            (
                (col_hbm, col),
                (x_hbm, xe.at[pl.ds(edge, rows)]),
                (cot_hbm, cot),
                (wmsg_hbm, wmsg),
                (wf_hbm, wf),
                (bf_hbm, bf),
                (ws_hbm, ws),
                (bs_hbm, bs),
                (gain_hbm, gain),
            )
        )
    ]
    cnt_loads = [pltpu.make_async_copy(cnt_hbm.at[b], cnt.at[b], cnt_sem.at[b]) for b in range(nb)]
    loads[0].start()
    for b in range(nb):
        cnt_loads[b].start()
    for load in loads[1:]:
        load.start()

    pay[...] = jnp.zeros_like(pay)
    dme[...] = jnp.zeros_like(dme)
    loads[0].wait()

    def build(b, carry):
        pltpu.make_async_copy(cnt_hbm.at[b], cnt.at[b], cnt_sem.at[b]).wait()
        tiles = [cnt[b, t].astype(jnp.float32).astype(jnp.bfloat16) for t in range(cnt.shape[1])]
        for d in range(SPAN):
            acc = tiles[0] if d == WIN else None
            for t in range(1, cnt.shape[1]):
                here = (col[b, t] - first_block - b + WIN == d).astype(jnp.float32)
                term = tiles[t] * jnp.full((blk, blk), here, jnp.float32).astype(jnp.bfloat16)
                acc = term if acc is None else acc + term
            band[b, :, d * blk : (d + 1) * blk] = acc
        return carry

    lax.fori_loop(0, nb, build, 0)
    pl.semaphore_wait(barrier, len(peers))

    halo_low = pltpu.make_async_remote_copy(
        src_ref=x_hbm.at[pl.ds(0, edge)], dst_ref=xe.at[pl.ds(edge + rows, edge)],
        send_sem=halo_s.at[0], recv_sem=halo_r.at[0], device_id=prv, device_id_type=MESH,
    )
    halo_high = pltpu.make_async_remote_copy(
        src_ref=x_hbm.at[pl.ds(rows - edge, edge)], dst_ref=xe.at[pl.ds(0, edge)],
        send_sem=halo_s.at[1], recv_sem=halo_r.at[1], device_id=nxt, device_id_type=MESH,
    )
    halo_low.start()
    halo_high.start()
    for load in loads[1:]:
        load.wait()

    size = GROUP * blk

    def process(b0):
        r0 = pl.multiple_of(b0 * blk, blk)
        here = pl.ds(r0, size)
        xs = xe[pl.ds(r0 + edge, size), :]
        agx = jnp.concatenate(
            [dot(band[b0 + g], xe[pl.ds(r0 + g * blk, SPAN * blk), :]) for g in range(GROUP)], axis=0
        ).astype(jnp.bfloat16)
        agg = dot(agx, wmsg[...]).astype(jnp.bfloat16)
        ph = dot(jnp.concatenate([xs, agg], axis=1), wf[...]) + bf[...]
        sg = jax.nn.sigmoid(ph)
        act = (ph * sg).astype(jnp.bfloat16)
        pn = dot(act, ws[...]) + bs[...]
        cen = pn - jnp.mean(pn, axis=-1, keepdims=True)
        inv = lax.rsqrt(jnp.mean(cen * cen, axis=-1, keepdims=True) + EPS)
        nrm = cen * inv
        upd_out[here, :] = (xs.astype(jnp.float32) + gain[...] * nrm).astype(jnp.bfloat16)
        c = cot[here, :].astype(jnp.float32)
        q = c * gain[...]
        dpn = (
            inv
            * (
                q
                - jnp.mean(q, axis=-1, keepdims=True)
                - nrm * jnp.mean(q * nrm, axis=-1, keepdims=True)
            )
        ).astype(jnp.bfloat16)
        dph = (dot_rt(dpn, ws[...]) * sg * (1.0 + ph * (1.0 - sg))).astype(jnp.bfloat16)
        dj = dot_rt(dph, wf[...])
        gsp[here, :] = c + dj[:, :blk]
        dag[here, :] = dj[:, blk:].astype(jnp.bfloat16)
        g1 = dot_lt(dph, jnp.concatenate([xs, agx], axis=1))
        pay[0:blk, :] += g1[:, :blk]
        pay[blk : 2 * blk, :] += g1[:, blk:]
        pay[2 * blk : 3 * blk, :] += dot_lt(act, dpn)
        pay[3 * blk : 3 * blk + 1, :] += jnp.sum(dph.astype(jnp.float32), axis=0, keepdims=True)
        pay[3 * blk + 1 : 3 * blk + 2, :] += jnp.sum(dpn.astype(jnp.float32), axis=0, keepdims=True)
        pay[3 * blk + 2 : 3 * blk + 3, :] += jnp.sum(c * nrm, axis=0, keepdims=True)

    def interior(i, carry):
        process(WIN + GROUP * i)
        return carry

    lax.fori_loop(0, (nb - 2 * WIN) // GROUP, interior, 0)
    halo_low.wait_recv()
    halo_high.wait_recv()

    def border(i, carry):
        process(i * (nb - WIN))
        return carry

    lax.fori_loop(0, 2, border, 0)

    order = (2, 1, 3, 0)
    quarters = [lax.rem(x + off, NX) for off in order]
    to_mate = []
    for j, q in enumerate(quarters):
        to_mate.append(
            pltpu.make_async_remote_copy(
                src_ref=pay.at[pl.ds(pl.multiple_of((1 - core) * HALF + q * QUARTER, PIECE), QUARTER)],
                dst_ref=r1.at[j], send_sem=c_s.at[j], recv_sem=c_r.at[j], device_id=mate, device_id_type=MESH,
            )
        )
        to_mate[-1].start()

    def scatter_row(b):
        r0 = pl.multiple_of(b * blk, blk)
        dme[pl.ds(r0, SPAN * blk), :] += dot_lt(band[b], dag[pl.ds(r0, blk), :])

    sends = list(to_mate)
    along_x = []
    for j, q in enumerate(quarters):
        to_mate[j].wait_recv()
        mine = pay[pl.ds(pl.multiple_of(core * HALF + q * QUARTER, PIECE), QUARTER), :]
        a1[j] = mine + r1[j]
        off = order[j]
        if off:
            copy = pltpu.make_async_remote_copy(
                src_ref=a1.at[j], dst_ref=r2.at[j],
                send_sem=x_s.at[j], recv_sem=x_r.at[j], device_id=at_x(off), device_id_type=MESH,
            )
            copy.start()
            along_x.append(copy)
    sends += along_x

    def border_rows(i, carry):
        b0 = i * (nb - WIN)
        for g in range(WIN):
            scatter_row(b0 + g)
        return carry

    lax.fori_loop(0, 2, border_rows, 0)
    bh_send[0] = dme[0:edge, :].astype(jnp.bfloat16)
    bh_send[1] = dme[edge + rows : 2 * edge + rows, :].astype(jnp.bfloat16)
    back_low = pltpu.make_async_remote_copy(
        src_ref=bh_send.at[0], dst_ref=bh_recv.at[0],
        send_sem=b_s.at[0], recv_sem=b_r.at[0], device_id=prv, device_id_type=MESH,
    )
    back_high = pltpu.make_async_remote_copy(
        src_ref=bh_send.at[1], dst_ref=bh_recv.at[1],
        send_sem=b_s.at[1], recv_sem=b_r.at[1], device_id=nxt, device_id_type=MESH,
    )
    back_low.start()
    back_high.start()
    sends += [halo_low, halo_high, back_low, back_high]

    for copy in along_x:
        copy.wait_recv()
    a2[...] = (a1[3] + r2[0]) + (r2[1] + r2[2])
    along_y = []
    for k in range(1, NY):
        copy = pltpu.make_async_remote_copy(
            src_ref=a2.at[pl.ds(pl.multiple_of(lax.rem(y + k, NY) * PIECE, PIECE), PIECE)],
            dst_ref=r3.at[k - 1],
            send_sem=y_s.at[k - 1], recv_sem=y_r.at[k - 1], device_id=at_y(k), device_id_type=MESH,
        )
        copy.start()
        along_y.append(copy)
    sends += along_y

    def inner_rows(b, carry):
        scatter_row(b)
        return carry

    lax.fori_loop(WIN, nb - WIN, inner_rows, 0)

    for copy in along_y:
        copy.wait_recv()
    total = a2[pl.ds(pl.multiple_of(y * PIECE, PIECE), PIECE), :]
    for k in range(1, NY):
        total = total + r3[k - 1]
    a3[...] = total
    r4[z] = total
    along_z = []
    for k in (6, 5, 7, 4, 8, 3, 9, 2, 10, 1, 11):
        copy = pltpu.make_async_remote_copy(
            src_ref=a3, dst_ref=r4.at[z],
            send_sem=z_s.at[k - 1], recv_sem=z_r.at[k - 1], device_id=at_z(k), device_id_type=MESH,
        )
        copy.start()
        along_z.append(copy)
    sends += along_z

    back_low.wait_recv()
    back_high.wait_recv()
    dme[edge : 2 * edge, :] += bh_recv[1].astype(jnp.float32)
    dme[rows : rows + edge, :] += bh_recv[0].astype(jnp.float32)

    def state_rows(i, carry):
        r0 = pl.multiple_of(i * size, size)
        here = pl.ds(r0, size)
        dm = dme[pl.ds(r0 + edge, size), :].astype(jnp.bfloat16)
        gs_out[here, :] = (gsp[here, :] + dot_rt(dm, wmsg[...])).astype(jnp.bfloat16)
        return carry

    lax.fori_loop(0, rows // size, state_rows, 0)

    for copy in along_z:
        copy.wait_recv()
    total = r4[0]
    for i in range(1, NZ):
        total = total + r4[i]
    half0 = core * HALF
    quarter0 = half0 + x * QUARTER
    own = pl.ds(pl.multiple_of(quarter0 + y * PIECE, PIECE), PIECE)
    out[own, :] = total
    gathers = []
    for k in range(1, NY):
        copy = pltpu.make_async_remote_copy(
            src_ref=out.at[own], dst_ref=out.at[own],
            send_sem=ay_s.at[k - 1], recv_sem=ay_r.at[k - 1], device_id=at_y(k), device_id_type=MESH,
        )
        copy.start()
        gathers.append(copy)
    for copy in gathers:
        copy.wait_recv()
    sends += gathers
    span = pl.ds(pl.multiple_of(quarter0, QUARTER), QUARTER)
    along_x = []
    for j, k in enumerate((2, 1, 3)):
        copy = pltpu.make_async_remote_copy(
            src_ref=out.at[span], dst_ref=out.at[span],
            send_sem=ax_s.at[j], recv_sem=ax_r.at[j], device_id=at_x(k), device_id_type=MESH,
        )
        copy.start()
        along_x.append(copy)
    sends += along_x
    shares = []
    for j, k in enumerate((0, 1, 3, 2)):
        if k:
            along_x[(2, 1, 3).index(k)].wait_recv()
        span = pl.ds(pl.multiple_of(half0 + lax.rem(x + NX - k, NX) * QUARTER, QUARTER), QUARTER)
        copy = pltpu.make_async_remote_copy(
            src_ref=out.at[span], dst_ref=out.at[span],
            send_sem=ac_s.at[j], recv_sem=ac_r.at[j], device_id=mate, device_id_type=MESH,
        )
        copy.start()
        shares.append(copy)
    sends += shares
    for copy in shares:
        copy.wait_recv()
    tot_out[...] = out[...]
    for copy in sends:
        copy.wait_send()


def finish_kernel(scale, upd_in, gs_in, tot, wmsg, wf, upd, gs, gwm, gwf, gb1, gws, gb2, gg):
    n = wmsg.shape[0]
    upd[...] = upd_in[...]
    gs[...] = gs_in[...]
    high = lax.Precision.HIGHEST
    s_t = tot[n : 2 * n, :]
    s = s_t.T
    low = wf[n:, :].astype(jnp.float32)
    gwm[...] = scale * lax.dot_general(
        s, low, (((1,), (1,)), ((), ())), precision=high, preferred_element_type=jnp.float32
    )
    gwf[0:n, :] = scale * tot[0:n, :].T
    gwf[n:, :] = scale * jnp.dot(
        wmsg[...].astype(jnp.float32).T, s, precision=high, preferred_element_type=jnp.float32
    )
    gws[...] = scale * tot[2 * n : 3 * n, :]
    gb1[...] = scale * tot[3 * n : 3 * n + 1, :]
    gb2[...] = scale * tot[3 * n + 1 : 3 * n + 2, :]
    gg[...] = scale * tot[3 * n + 2 : 3 * n + 3, :]


def shards(
    node_state, w_msg, w_first, b_first, w_second, b_second, ln_gain, col_index, edge_counts, cotangent
):
    rows, hid = node_state.shape
    nb, tiles, blk, _ = edge_counts.shape
    ext = rows + 2 * WIN * blk
    devices = lax.axis_size("dom") * lax.axis_size("feat")
    scale = 1.0 / math.sqrt(rows * devices)
    f32, bf16 = jnp.float32, jnp.bfloat16
    vmem, sem = pltpu.VMEM, pltpu.SemaphoreType.DMA
    anywhere = pl.BlockSpec(memory_space=pl.ANY)
    whole = pl.BlockSpec(memory_space=pltpu.VMEM)
    shape = jax.ShapeDtypeStruct
    upd, gs, tot = pl.pallas_call(
        layer_kernel,
        out_shape=(shape((rows, hid), bf16), shape((rows, hid), bf16), shape((TOTAL, hid), f32)),
        in_specs=[anywhere] * 10,
        out_specs=(whole,) * 3,
        scratch_shapes=[
            vmem((ext, hid), bf16), vmem((hid, hid), bf16), vmem((2 * hid, hid), bf16), vmem((1, hid), f32),
            vmem((hid, hid), bf16), vmem((1, hid), f32), vmem((1, hid), f32), pltpu.SMEM((nb, tiles), jnp.int32),
            vmem((nb, tiles, blk, blk), jnp.int32), vmem((rows, hid), bf16),
            vmem((nb, blk, SPAN * blk), bf16), vmem((rows, hid), bf16), vmem((rows, hid), f32), vmem((ext, hid), f32),
            vmem((TOTAL, hid), f32), vmem((NX, QUARTER, hid), f32), vmem((NX, QUARTER, hid), f32),
            vmem((NX - 1, QUARTER, hid), f32), vmem((QUARTER, hid), f32), vmem((NY - 1, PIECE, hid), f32),
            vmem((PIECE, hid), f32), vmem((NZ, PIECE, hid), f32), vmem((TOTAL, hid), f32),
            vmem((2, WIN * blk, hid), bf16), vmem((2, WIN * blk, hid), bf16),
            sem((9,)), sem((nb,)), sem((2,)), sem((2,)), sem((4,)), sem((4,)), sem((3,)), sem((3,)),
            sem((7,)), sem((7,)), sem((11,)), sem((11,)), sem((7,)), sem((7,)), sem((3,)), sem((3,)),
            sem((4,)), sem((4,)), sem((2,)), sem((2,)),
        ],
        compiler_params=pltpu.CompilerParams(
            collective_id=0, has_side_effects=True, vmem_limit_bytes=48 * 1024 * 1024
        ),
        name="layer",
    )(
        node_state, w_msg, w_first, b_first.reshape(1, hid), w_second, b_second.reshape(1, hid),
        ln_gain.reshape(1, hid), col_index, edge_counts, cotangent,
    )
    row = shape((1, hid), f32)
    upd, gs, gwm, gwf, gb1, gws, gb2, gg = pl.pallas_call(
        functools.partial(finish_kernel, scale),
        out_shape=(
            shape((rows, hid), bf16), shape((rows, hid), bf16), shape((hid, hid), f32),
            shape((2 * hid, hid), f32), row, shape((hid, hid), f32), row, row,
        ),
        in_specs=[whole] * 5,
        out_specs=(whole,) * 8,
        name="finish",
    )(upd, gs, tot, w_msg, w_first)
    return (upd, gs, gwm, gwf, gb1.reshape(hid), gws, gb2.reshape(hid), gg.reshape(hid))


def solution(mesh):
    nodes = P(("dom", "feat"), None)
    return jax.shard_map(
        shards,
        mesh=mesh,
        in_specs=(nodes, P(), P(), P(), P(), P(), P(), nodes, P(("dom", "feat"), None, None, None), nodes),
        out_specs=(nodes, nodes, P(), P(), P(), P(), P(), P()),
        check_vma=False,
    )
```

time: 667 us -> 71.1 us (0.11)
  waiting for transfers between devices: 472 us -> 0 us
  blocking collectives: 111 us -> 0 us
  Pallas kernels: 0 us -> 58.8 us
  starting transfers between devices: 31.5 us -> 0 us
  between operations: 14.4 us -> 0.66 us
  matrix products: 13 us -> 0 us
  local copies, waits for them, and re-layouts: 20.1 us -> 11.2 us
    psum x1 -> x0, waiting for transfers between devices: 472 us -> none  [shards(): lax.psum((terms[0], terms[1], terms[2], terms[3], terms[4], terms[5]), ('...]
    psum x1 -> x0, blocking collectives: 111 us -> none  [shards(): lax.psum((terms[0], terms[1], terms[2], terms[3], terms[4], terms[5]), ('...]
    pallas_call x0 -> x2, Pallas kernels: none -> 58.8 us  [the longest x1 56.4 us: shards(): pl.pallas_call(layer_kernel, out_shape=(shape((rows, hid), bf16), shape((...]
    ppermute x4 -> x0, starting transfers between devices: 31.5 us -> none  [the longest x1 15.8 us: with_halo(): lax.ppermute(head, axis, [((i + 1) % count, i) for i in range(ends)])]
    dot_general x12 -> x0, matrix products: 13 us -> none  [the longest x1 4.34 us: shards(): jnp.einsum('btc,btjh->cjh', one_hot, contribution, precision=lax.Precisio...]
  transfers between devices with their start and end apart: 5 -> 0, of which waited for: 1 -> 0; matrix products, arithmetic and copies ran while one was open for 1% -> 0% of each run, Pallas kernels for 0% -> 0%
where the time goes in v1:
time: 71.1 us; the launch traced here: 70.6 us
  Pallas kernels  58.8 us (83%)
  local copies, waits for them, and re-layouts  11.2 us (16%)
    pallas_call x1, Pallas kernels, shards(): pl.pallas_call(layer_kernel, out_shape=(shape((rows, hid), bf16), shape((...  56.4 us
    unnamed x25, local copies, waits for them, and re-layouts  11.2 us
    pallas_call x1, Pallas kernels, shards(): pl.pallas_call(functools.partial(finish_kernel, scale), out_shape=(shape(...  2.43 us

profile of v1, /device:TPU:1, one launch (start us, length us, event | category | flops | bytes accessed | tf_op | source)
XLA Modules:
  0.0 70.6 jit_solution(15211436430087045050)
XLA Ops:
  0.6 0.8 %copy.18.col_hbm = s32[12,4]{1,0:T(8,128)S(1)} copy(s32[12,4]{0,1:T(4,128)} %param.17) | data formatting | bytes 384 | tf_op args[7]
  1.4 0.0 copy-start
  1.4 1.9 %copy-done = s32[12,4,128,128]{3,2,1,0:T(8,128)S(1)} copy-done((s32[12,4,128,128]{3,2,1,0:T(8,128)S(1)}, s32[12,4,128,128]{3,2,1,0:T(8,128)}, u32[]{:S(2)}) %copy-start) | copy-done | bytes 3145752
  3.3 0.0 copy-start.1
  3.3 1.0 %copy-done.1 = bf16[1536,128]{1,0:T(8,128)(2,1)S(1)} copy-done((bf16[1536,128]{1,0:T(8,128)(2,1)S(1)}, bf16[1536,128]{1,0:T(8,128)(2,1)}, u32[]{:S(2)}) %copy-start.1) | copy-done | bytes 393240
  4.3 0.0 copy-start.2
  4.3 1.0 %copy-done.2 = bf16[1536,128]{1,0:T(8,128)(2,1)S(1)} copy-done((bf16[1536,128]{1,0:T(8,128)(2,1)S(1)}, bf16[1536,128]{1,0:T(8,128)(2,1)}, u32[]{:S(2)}) %copy-start.2) | copy-done | bytes 393240
  5.3 0.0 copy-start.5
  5.3 0.8 %copy-done.5 = bf16[256,128]{1,0:T(8,128)(2,1)S(1)} copy-done((bf16[256,128]{1,0:T(8,128)(2,1)S(1)}, bf16[256,128]{1,0:T(8,128)(2,1)}, u32[]{:S(2)}) %copy-start.5) | copy-done | bytes 65560
  6.1 0.0 copy-start.7
  6.1 0.8 %copy-done.7 = bf16[128,128]{1,0:T(8,128)(2,1)S(1)} copy-done((bf16[128,128]{1,0:T(8,128)(2,1)S(1)}, bf16[128,128]{1,0:T(8,128)(2,1)}, u32[]{:S(2)}) %copy-start.7) | copy-done | bytes 32792
  6.9 0.0 copy-start.8
  6.9 0.8 %copy-done.8 = bf16[128,128]{1,0:T(8,128)(2,1)S(1)} copy-done((bf16[128,128]{1,0:T(8,128)(2,1)S(1)}, bf16[128,128]{1,0:T(8,128)(2,1)}, u32[]{:S(2)}) %copy-start.8) | copy-done | bytes 32792
  7.6 0.0 copy-start.9
  7.6 0.7 copy-done.9
  8.3 0.0 copy-start.10
  8.3 0.7 copy-done.10
  9.0 0.0 copy-start.11
  9.0 0.7 copy-done.11
  9.6 56.4 %layer.1 = (bf16[1536,128]{1,0:T(8,128)(2,1)S(1)}, bf16[1536,128]{1,0:T(8,128)(2,1)S(1)}, f32[512,128]{1,0:T(8,128)S(1)}) custom-call(bf16[1536,128]{1,0:T(8,128)(2,1)S(1)} %copy-done.1, bf16[128,128]{1,0:T(8,128)(2,1)S(1)} %copy-done.7, bf16[256,128]{1,0:T(8,128)(2,1)S(1)} %copy-done.5, f32[1,128]{1,0:T(1,128)S(1)} %bitcast.6, ...), custom_call_target="tpu_custom_call" | custom-call | tf_op jit(solution)/shard_map/layer/pallas_call | solution.py:378
  66.0 0.0 copy-start.3
  66.0 0.7 %copy-done.3 = bf16[1536,128]{1,0:T(8,128)(2,1)} copy-done((bf16[1536,128]{1,0:T(8,128)(2,1)}, bf16[1536,128]{1,0:T(8,128)(2,1)S(1)}, u32[]{:S(2)}) %copy-start.3) | copy-done | bytes 393240
  66.7 0.0 copy-start.4
  66.7 0.7 %copy-done.4 = bf16[1536,128]{1,0:T(8,128)(2,1)} copy-done((bf16[1536,128]{1,0:T(8,128)(2,1)}, bf16[1536,128]{1,0:T(8,128)(2,1)S(1)}, u32[]{:S(2)}) %copy-start.4) | copy-done | bytes 393240
  67.5 0.0 copy-start.6
  67.5 0.7 %copy-done.6 = f32[512,128]{1,0:T(8,128)} copy-done((f32[512,128]{1,0:T(8,128)}, f32[512,128]{1,0:T(8,128)S(1)}, u32[]{:S(2)}) %copy-start.6) | copy-done | bytes 262168
  68.2 2.4 %finish.1 = (bf16[1536,128]{1,0:T(8,128)(2,1)}, bf16[1536,128]{1,0:T(8,128)(2,1)}, f32[128,128]{1,0:T(8,128)}, f32[256,128]{1,0:T(8,128)}, f32[1,128]{1,0:T(1,12...) custom-call(bf16[1536,128]{1,0:T(8,128)(2,1)} %copy-done.3, bf16[1536,128]{1,0:T(8,128)(2,1)} %copy-done.4, ...), custom_call_target="tpu_custom_call" | custom-call | tf_op jit(solution)/shard_map/finish/pallas_call | solution.py:405
Async XLA Ops:
  1.4 1.9 %copy-start = (s32[12,4,128,128]{3,2,1,0:T(8,128)S(1)}, s32[12,4,128,128]{3,2,1,0:T(8,128)}, u32[]{:S(2)}) copy-start(s32[12,4,128,128]{3,2,1,0:T(8,128)} %cnt_hbm.1) | copy-start | bytes 9437188
  3.3 1.0 %copy-start.1 = (bf16[1536,128]{1,0:T(8,128)(2,1)S(1)}, bf16[1536,128]{1,0:T(8,128)(2,1)}, u32[]{:S(2)}) copy-start(bf16[1536,128]{1,0:T(8,128)(2,1)} %x_hbm.1) | copy-start | bytes 1179652
  4.3 1.0 %copy-start.2 = (bf16[1536,128]{1,0:T(8,128)(2,1)S(1)}, bf16[1536,128]{1,0:T(8,128)(2,1)}, u32[]{:S(2)}) copy-start(bf16[1536,128]{1,0:T(8,128)(2,1)} %cot_hbm.1) | copy-start | bytes 1179652
  5.3 0.8 %copy-start.5 = (bf16[256,128]{1,0:T(8,128)(2,1)S(1)}, bf16[256,128]{1,0:T(8,128)(2,1)}, u32[]{:S(2)}) copy-start(bf16[256,128]{1,0:T(8,128)(2,1)} %wf.1) | copy-start | bytes 196612
  6.1 0.8 %copy-start.7 = (bf16[128,128]{1,0:T(8,128)(2,1)S(1)}, bf16[128,128]{1,0:T(8,128)(2,1)}, u32[]{:S(2)}) copy-start(bf16[128,128]{1,0:T(8,128)(2,1)} %wmsg.1) | copy-start | bytes 98308
  6.9 0.8 %copy-start.8 = (bf16[128,128]{1,0:T(8,128)(2,1)S(1)}, bf16[128,128]{1,0:T(8,128)(2,1)}, u32[]{:S(2)}) copy-start(bf16[128,128]{1,0:T(8,128)(2,1)} %ws_hbm.1) | copy-start | bytes 98308
  7.6 0.7 copy-start.9
  8.3 0.7 copy-start.10
  9.0 0.7 copy-start.11
  66.0 0.7 %copy-start.3 = (bf16[1536,128]{1,0:T(8,128)(2,1)}, bf16[1536,128]{1,0:T(8,128)(2,1)S(1)}, u32[]{:S(2)}) copy-start(bf16[1536,128]{1,0:T(8,128)(2,1)S(1)} %get-tuple-element.19.upd_in) | copy-start | bytes 1179652
  66.7 0.7 %copy-start.4 = (bf16[1536,128]{1,0:T(8,128)(2,1)}, bf16[1536,128]{1,0:T(8,128)(2,1)S(1)}, u32[]{:S(2)}) copy-start(bf16[1536,128]{1,0:T(8,128)(2,1)S(1)} %get-tuple-element.20.gs_in) | copy-start | bytes 1179652
  67.5 0.7 %copy-start.6 = (f32[512,128]{1,0:T(8,128)}, f32[512,128]{1,0:T(8,128)S(1)}, u32[]{:S(2)}) copy-start(f32[512,128]{1,0:T(8,128)S(1)} %get-tuple-element.21.tot) | copy-start | bytes 786436

commit v2 on v1

--- a/solution.py
+++ b/solution.py
@@ -33,14 +33,16 @@
 
 
 def layer_kernel(
+    scale,
     x_hbm, wmsg_hbm, wf_hbm, bf_hbm, ws_hbm, bs_hbm, gain_hbm, col_hbm, cnt_hbm, cot_hbm,
-    upd_out, gs_out, tot_out,
-    xe, wmsg, wf, bf, ws, bs, gain, col, cnt, cot,
+    upd_out, gs_out, gwm_out, gwf_out, gb1_out, gws_out, gb2_out, gg_out,
+    xe, wmsg, wmsg_t, wf, bf, ws, bs, gain, col, cnt, cot,
     band, dag, gsp, dme, pay, r1, a1, r2, a2, r3, a3, r4, out, bh_send, bh_recv,
     in_sem, cnt_sem, halo_s, halo_r, c_s, c_r, x_s, x_r, y_s, y_r, z_s, z_r,
     ay_s, ay_r, ax_s, ax_r, ac_s, ac_r, b_s, b_r,
 ):
     nb = cnt_hbm.shape[0]
+    hid = x_hbm.shape[1]
     rows = x_hbm.shape[0]
     blk = cnt_hbm.shape[2]
     edge = WIN * blk
@@ -112,7 +114,7 @@
         for d in range(SPAN):
             acc = tiles[0] if d == WIN else None
             for t in range(1, cnt.shape[1]):
-                here = (col[b, t] - first_block - b + WIN == d).astype(jnp.float32)
+                here = (col[t, b] - first_block - b + WIN == d).astype(jnp.float32)
                 term = tiles[t] * jnp.full((blk, blk), here, jnp.float32).astype(jnp.bfloat16)
                 acc = term if acc is None else acc + term
             band[b, :, d * blk : (d + 1) * blk] = acc
@@ -134,6 +136,7 @@
     for load in loads[1:]:
         load.wait()
 
+    wmsg_t[...] = wmsg[...].T
     size = GROUP * blk
 
     def process(b0):
@@ -166,9 +169,8 @@
         dj = dot_rt(dph, wf[...])
         gsp[here, :] = c + dj[:, :blk]
         dag[here, :] = dj[:, blk:].astype(jnp.bfloat16)
-        g1 = dot_lt(dph, jnp.concatenate([xs, agx], axis=1))
-        pay[0:blk, :] += g1[:, :blk]
-        pay[blk : 2 * blk, :] += g1[:, blk:]
+        pay[0:blk, :] += dot_lt(xs, dph)
+        pay[blk : 2 * blk, :] += dot_lt(agx, dph)
         pay[2 * blk : 3 * blk, :] += dot_lt(act, dpn)
         pay[3 * blk : 3 * blk + 1, :] += jnp.sum(dph.astype(jnp.float32), axis=0, keepdims=True)
         pay[3 * blk + 1 : 3 * blk + 2, :] += jnp.sum(dpn.astype(jnp.float32), axis=0, keepdims=True)
@@ -266,6 +268,7 @@
     total = a2[pl.ds(pl.multiple_of(y * PIECE, PIECE), PIECE), :]
     for k in range(1, NY):
         total = total + r3[k - 1]
+    total = total * scale
     a3[...] = total
     r4[z] = total
     along_z = []
@@ -336,30 +339,32 @@
     sends += shares
     for copy in shares:
         copy.wait_recv()
-    tot_out[...] = out[...]
+    grad_s = out[hid : 2 * hid, :]
+    part1 = grad_s.astype(jnp.bfloat16)
+    rest = grad_s - part1.astype(jnp.float32)
+    part2 = rest.astype(jnp.bfloat16)
+    part3 = (rest - part2.astype(jnp.float32)).astype(jnp.bfloat16)
+    low = wf[hid:, :]
+    gwm_out[...] = (dot_rt(part3, low) + dot_rt(part2, low)) + dot_rt(part1, low)
+    gwf_out[0:hid, :] = out[0:hid, :]
+    turned = wmsg_t[...]
+    gwf_out[hid:, :] = (dot(turned, part3) + dot(turned, part2)) + dot(turned, part1)
+    gws_out[...] = out[2 * hid : 3 * hid, :]
+    gb1_out[...] = out[3 * hid : 3 * hid + 1, :]
+    gb2_out[...] = out[3 * hid + 1 : 3 * hid + 2, :]
+    gg_out[...] = out[3 * hid + 2 : 3 * hid + 3, :]
     for copy in sends:
         copy.wait_send()
 
 
-def finish_kernel(scale, upd_in, gs_in, tot, wmsg, wf, upd, gs, gwm, gwf, gb1, gws, gb2, gg):
-    n = wmsg.shape[0]
-    upd[...] = upd_in[...]
-    gs[...] = gs_in[...]
-    high = lax.Precision.HIGHEST
-    s_t = tot[n : 2 * n, :]
-    s = s_t.T
-    low = wf[n:, :].astype(jnp.float32)
-    gwm[...] = scale * lax.dot_general(
-        s, low, (((1,), (1,)), ((), ())), precision=high, preferred_element_type=jnp.float32
-    )
-    gwf[0:n, :] = scale * tot[0:n, :].T
-    gwf[n:, :] = scale * jnp.dot(
-        wmsg[...].astype(jnp.float32).T, s, precision=high, preferred_element_type=jnp.float32
-    )
-    gws[...] = scale * tot[2 * n : 3 * n, :]
-    gb1[...] = scale * tot[3 * n : 3 * n + 1, :]
-    gb2[...] = scale * tot[3 * n + 1 : 3 * n + 2, :]
-    gg[...] = scale * tot[3 * n + 2 : 3 * n + 3, :]
+def finish_kernel(*refs):
+    count = (len(refs) - 1) // 2
+    sem = refs[-1]
+    copies = [pltpu.make_async_copy(refs[i], refs[count + i], sem.at[i]) for i in range(count)]
+    for copy in copies:
+        copy.start()
+    for copy in copies:
+        copy.wait()
 
 
 def shards(
@@ -372,17 +377,22 @@
     scale = 1.0 / math.sqrt(rows * devices)
     f32, bf16 = jnp.float32, jnp.bfloat16
     vmem, sem = pltpu.VMEM, pltpu.SemaphoreType.DMA
-    anywhere = pl.BlockSpec(memory_space=pl.ANY)
+    in_hbm = pl.BlockSpec(memory_space=pltpu.HBM)
     whole = pl.BlockSpec(memory_space=pltpu.VMEM)
     shape = jax.ShapeDtypeStruct
-    upd, gs, tot = pl.pallas_call(
-        layer_kernel,
-        out_shape=(shape((rows, hid), bf16), shape((rows, hid), bf16), shape((TOTAL, hid), f32)),
-        in_specs=[anywhere] * 10,
-        out_specs=(whole,) * 3,
+    row = shape((1, hid), f32)
+    results = (
+        shape((rows, hid), bf16), shape((rows, hid), bf16), shape((hid, hid), f32),
+        shape((2 * hid, hid), f32), row, shape((hid, hid), f32), row, row,
+    )
+    results = pl.pallas_call(
+        functools.partial(layer_kernel, scale),
+        out_shape=results,
+        in_specs=[in_hbm] * 10,
+        out_specs=(whole,) * 8,
         scratch_shapes=[
-            vmem((ext, hid), bf16), vmem((hid, hid), bf16), vmem((2 * hid, hid), bf16), vmem((1, hid), f32),
-            vmem((hid, hid), bf16), vmem((1, hid), f32), vmem((1, hid), f32), pltpu.SMEM((nb, tiles), jnp.int32),
+            vmem((ext, hid), bf16), vmem((hid, hid), bf16), vmem((hid, hid), bf16), vmem((2 * hid, hid), bf16), vmem((1, hid), f32),
+            vmem((hid, hid), bf16), vmem((1, hid), f32), vmem((1, hid), f32), pltpu.SMEM((tiles, nb), jnp.int32),
             vmem((nb, tiles, blk, blk), jnp.int32), vmem((rows, hid), bf16),
             vmem((nb, blk, SPAN * blk), bf16), vmem((rows, hid), bf16), vmem((rows, hid), f32), vmem((ext, hid), f32),
             vmem((TOTAL, hid), f32), vmem((NX, QUARTER, hid), f32), vmem((NX, QUARTER, hid), f32),
@@ -394,24 +404,27 @@
             sem((4,)), sem((4,)), sem((2,)), sem((2,)),
         ],
         compiler_params=pltpu.CompilerParams(
-            collective_id=0, has_side_effects=True, vmem_limit_bytes=48 * 1024 * 1024
+            collective_id=0, has_side_effects=True, vmem_limit_bytes=32 * 1024 * 1024
         ),
         name="layer",
     )(
-        node_state, w_msg, w_first, b_first.reshape(1, hid), w_second, b_second.reshape(1, hid),
-        ln_gain.reshape(1, hid), col_index, edge_counts, cotangent,
-    )
-    row = shape((1, hid), f32)
+        *[
+            pltpu.with_memory_space_constraint(a, pltpu.HBM)
+            for a in (
+                node_state, w_msg, w_first, b_first.reshape(1, hid), w_second, b_second.reshape(1, hid),
+                ln_gain.reshape(1, hid), col_index.T, edge_counts, cotangent,
+            )
+        ]
+    )
     upd, gs, gwm, gwf, gb1, gws, gb2, gg = pl.pallas_call(
-        functools.partial(finish_kernel, scale),
-        out_shape=(
-            shape((rows, hid), bf16), shape((rows, hid), bf16), shape((hid, hid), f32),
-            shape((2 * hid, hid), f32), row, shape((hid, hid), f32), row, row,
-        ),
-        in_specs=[whole] * 5,
-        out_specs=(whole,) * 8,
+        finish_kernel,
+        out_shape=tuple(shape(r.shape, r.dtype) for r in results),
+        in_specs=[whole] * 8,
+        out_specs=(in_hbm,) * 8,
+        scratch_shapes=[sem((8,))],
+        compiler_params=pltpu.CompilerParams(vmem_limit_bytes=4 * 1024 * 1024),
         name="finish",
-    )(upd, gs, tot, w_msg, w_first)
+    )(*results)
     return (upd, gs, gwm, gwf, gb1.reshape(hid), gws, gb2.reshape(hid), gg.reshape(hid))
 
 

time: 71.1 us -> 58.6 us (0.82)
  local copies, waits for them, and re-layouts: 11.2 us -> 0 us
  Pallas kernels: 58.8 us -> 57.8 us
    unnamed x25 -> x0, local copies, waits for them, and re-layouts: 11.2 us -> none
    pallas_call x2, Pallas kernels: 58.8 us -> 57.8 us  [the longest x1 56.7 us: shards(): pl.pallas_call(functools.partial(layer_kernel, scale), out_shape=results,...]
where the time goes in v2:
time: 58.6 us; the launch traced here: 58.4 us
  Pallas kernels  57.8 us (99%)
  between operations  0.64 us (1%)
    pallas_call x1, Pallas kernels, shards(): pl.pallas_call(functools.partial(layer_kernel, scale), out_shape=results,...  56.7 us

profile of v2, /device:TPU:1, one launch (start us, length us, event | category | flops | bytes accessed | tf_op | source)
XLA Modules:
  0.0 58.4 jit_solution(16785604656122689450)
XLA Ops:
  0.6 56.7 %layer.1 = (bf16[1536,128]{1,0:T(8,128)(2,1)S(1)}, bf16[1536,128]{1,0:T(8,128)(2,1)S(1)}, f32[128,128]{1,0:T(8,128)S(1)}, f32[256,128]{1,0:T(8,128)S(1)}, f32[1,...) custom-call(bf16[1536,128]{1,0:T(8,128)(2,1)} %x_hbm.1, ...), custom_call_target="tpu_custom_call" | custom-call | tf_op jit(solution)/shard_map/layer/pallas_call | solution.py:388
  57.4 1.0 %finish.1 = (bf16[1536,128]{1,0:T(8,128)(2,1)}, bf16[1536,128]{1,0:T(8,128)(2,1)}, f32[128,128]{1,0:T(8,128)}, f32[256,128]{1,0:T(8,128)}, f32[1,128]{1,0:T(1,12...) custom-call(bf16[1536,128]{1,0:T(8,128)(2,1)S(1)} %get-tuple-element.24.refs_0_, ...), custom_call_target="tpu_custom_call" | custom-call | tf_op jit(solution)/shard_map/finish/pallas_call | solution.py:419

commit v3 on v2

--- a/solution.py
+++ b/solution.py
@@ -37,7 +37,7 @@
     x_hbm, wmsg_hbm, wf_hbm, bf_hbm, ws_hbm, bs_hbm, gain_hbm, col_hbm, cnt_hbm, cot_hbm,
     upd_out, gs_out, gwm_out, gwf_out, gb1_out, gws_out, gb2_out, gg_out,
     xe, wmsg, wmsg_t, wf, bf, ws, bs, gain, col, cnt, cot,
-    band, dag, gsp, dme, pay, r1, a1, r2, a2, r3, a3, r4, out, bh_send, bh_recv,
+    band, dag, gsp, dme, pay, pay_b, r1, a1, r2, a2, a2_b, r3, a3, r4, out, bh_send, bh_recv,
     in_sem, cnt_sem, halo_s, halo_r, c_s, c_r, x_s, x_r, y_s, y_r, z_s, z_r,
     ay_s, ay_r, ax_s, ax_r, ac_s, ac_r, b_s, b_r,
 ):
@@ -192,11 +192,12 @@
 
     order = (2, 1, 3, 0)
     quarters = [lax.rem(x + off, NX) for off in order]
+    pay_b[...] = pay[...].astype(jnp.bfloat16)
     to_mate = []
     for j, q in enumerate(quarters):
         to_mate.append(
             pltpu.make_async_remote_copy(
-                src_ref=pay.at[pl.ds(pl.multiple_of((1 - core) * HALF + q * QUARTER, PIECE), QUARTER)],
+                src_ref=pay_b.at[pl.ds(pl.multiple_of((1 - core) * HALF + q * QUARTER, QUARTER), QUARTER)],
                 dst_ref=r1.at[j], send_sem=c_s.at[j], recv_sem=c_r.at[j], device_id=mate, device_id_type=MESH,
             )
         )
@@ -210,10 +211,11 @@
     along_x = []
     for j, q in enumerate(quarters):
         to_mate[j].wait_recv()
-        mine = pay[pl.ds(pl.multiple_of(core * HALF + q * QUARTER, PIECE), QUARTER), :]
-        a1[j] = mine + r1[j]
+        mine = pay[pl.ds(pl.multiple_of(core * HALF + q * QUARTER, QUARTER), QUARTER), :]
+        part = mine + r1[j].astype(jnp.float32)
         off = order[j]
         if off:
+            a1[j] = part.astype(jnp.bfloat16)
             copy = pltpu.make_async_remote_copy(
                 src_ref=a1.at[j], dst_ref=r2.at[j],
                 send_sem=x_s.at[j], recv_sem=x_r.at[j], device_id=at_x(off), device_id_type=MESH,
@@ -245,11 +247,14 @@
 
     for copy in along_x:
         copy.wait_recv()
-    a2[...] = (a1[3] + r2[0]) + (r2[1] + r2[2])
+    part = part + (r2[0].astype(jnp.float32) + (r2[1].astype(jnp.float32) + r2[2].astype(jnp.float32)))
+    part = part.reshape(NY, PIECE, hid)
+    a2[...] = part
+    a2_b[...] = part.astype(jnp.bfloat16)
     along_y = []
     for k in range(1, NY):
         copy = pltpu.make_async_remote_copy(
-            src_ref=a2.at[pl.ds(pl.multiple_of(lax.rem(y + k, NY) * PIECE, PIECE), PIECE)],
+            src_ref=a2_b.at[lax.rem(y + k, NY)],
             dst_ref=r3.at[k - 1],
             send_sem=y_s.at[k - 1], recv_sem=y_r.at[k - 1], device_id=at_y(k), device_id_type=MESH,
         )
@@ -265,10 +270,10 @@
 
     for copy in along_y:
         copy.wait_recv()
-    total = a2[pl.ds(pl.multiple_of(y * PIECE, PIECE), PIECE), :]
+    total = a2[y]
     for k in range(1, NY):
-        total = total + r3[k - 1]
-    total = total * scale
+        total = total + r3[k - 1].astype(jnp.float32)
+    total = (total * scale).astype(jnp.bfloat16)
     a3[...] = total
     r4[z] = total
     along_z = []
@@ -297,13 +302,13 @@
 
     for copy in along_z:
         copy.wait_recv()
-    total = r4[0]
+    total = r4[0].astype(jnp.float32)
     for i in range(1, NZ):
-        total = total + r4[i]
-    half0 = core * HALF
-    quarter0 = half0 + x * QUARTER
-    own = pl.ds(pl.multiple_of(quarter0 + y * PIECE, PIECE), PIECE)
-    out[own, :] = total
+        total = total + r4[i].astype(jnp.float32)
+    half0 = core * (NX * NY)
+    quarter0 = half0 + x * NY
+    own = quarter0 + y
+    out[own] = total.astype(jnp.bfloat16)
     gathers = []
     for k in range(1, NY):
         copy = pltpu.make_async_remote_copy(
@@ -315,7 +320,7 @@
     for copy in gathers:
         copy.wait_recv()
     sends += gathers
-    span = pl.ds(pl.multiple_of(quarter0, QUARTER), QUARTER)
+    span = pl.ds(quarter0, NY)
     along_x = []
     for j, k in enumerate((2, 1, 3)):
         copy = pltpu.make_async_remote_copy(
@@ -329,7 +334,7 @@
     for j, k in enumerate((0, 1, 3, 2)):
         if k:
             along_x[(2, 1, 3).index(k)].wait_recv()
-        span = pl.ds(pl.multiple_of(half0 + lax.rem(x + NX - k, NX) * QUARTER, QUARTER), QUARTER)
+        span = pl.ds(half0 + lax.rem(x + NX - k, NX) * NY, NY)
         copy = pltpu.make_async_remote_copy(
             src_ref=out.at[span], dst_ref=out.at[span],
             send_sem=ac_s.at[j], recv_sem=ac_r.at[j], device_id=mate, device_id_type=MESH,
@@ -339,20 +344,15 @@
     sends += shares
     for copy in shares:
         copy.wait_recv()
-    grad_s = out[hid : 2 * hid, :]
-    part1 = grad_s.astype(jnp.bfloat16)
-    rest = grad_s - part1.astype(jnp.float32)
-    part2 = rest.astype(jnp.bfloat16)
-    part3 = (rest - part2.astype(jnp.float32)).astype(jnp.bfloat16)
-    low = wf[hid:, :]
-    gwm_out[...] = (dot_rt(part3, low) + dot_rt(part2, low)) + dot_rt(part1, low)
-    gwf_out[0:hid, :] = out[0:hid, :]
-    turned = wmsg_t[...]
-    gwf_out[hid:, :] = (dot(turned, part3) + dot(turned, part2)) + dot(turned, part1)
-    gws_out[...] = out[2 * hid : 3 * hid, :]
-    gb1_out[...] = out[3 * hid : 3 * hid + 1, :]
-    gb2_out[...] = out[3 * hid + 1 : 3 * hid + 2, :]
-    gg_out[...] = out[3 * hid + 2 : 3 * hid + 3, :]
+    total = out[...].astype(jnp.float32).reshape(TOTAL, hid)
+    grad_s = total[hid : 2 * hid].astype(jnp.bfloat16)
+    gwm_out[...] = dot_rt(grad_s, wf[hid:, :])
+    gwf_out[0:hid, :] = total[0:hid]
+    gwf_out[hid:, :] = dot(wmsg_t[...], grad_s)
+    gws_out[...] = total[2 * hid : 3 * hid]
+    gb1_out[...] = total[3 * hid : 3 * hid + 1]
+    gb2_out[...] = total[3 * hid + 1 : 3 * hid + 2]
+    gg_out[...] = total[3 * hid + 2 : 3 * hid + 3]
     for copy in sends:
         copy.wait_send()
 
@@ -395,9 +395,10 @@
             vmem((hid, hid), bf16), vmem((1, hid), f32), vmem((1, hid), f32), pltpu.SMEM((tiles, nb), jnp.int32),
             vmem((nb, tiles, blk, blk), jnp.int32), vmem((rows, hid), bf16),
             vmem((nb, blk, SPAN * blk), bf16), vmem((rows, hid), bf16), vmem((rows, hid), f32), vmem((ext, hid), f32),
-            vmem((TOTAL, hid), f32), vmem((NX, QUARTER, hid), f32), vmem((NX, QUARTER, hid), f32),
-            vmem((NX - 1, QUARTER, hid), f32), vmem((QUARTER, hid), f32), vmem((NY - 1, PIECE, hid), f32),
-            vmem((PIECE, hid), f32), vmem((NZ, PIECE, hid), f32), vmem((TOTAL, hid), f32),
+            vmem((TOTAL, hid), f32), vmem((TOTAL, hid), bf16), vmem((NX, QUARTER, hid), bf16),
+            vmem((NX, QUARTER, hid), bf16), vmem((NX - 1, QUARTER, hid), bf16), vmem((NY, PIECE, hid), f32),
+            vmem((NY, PIECE, hid), bf16), vmem((NY - 1, PIECE, hid), bf16), vmem((PIECE, hid), bf16),
+            vmem((NZ, PIECE, hid), bf16), vmem((TOTAL // PIECE, PIECE, hid), bf16),
             vmem((2, WIN * blk, hid), bf16), vmem((2, WIN * blk, hid), bf16),
             sem((9,)), sem((nb,)), sem((2,)), sem((2,)), sem((4,)), sem((4,)), sem((3,)), sem((3,)),
             sem((7,)), sem((7,)), sem((11,)), sem((11,)), sem((7,)), sem((7,)), sem((3,)), sem((3,)),

time: 58.6 us -> 57.3 us (0.978)
  Pallas kernels: 57.8 us -> 56.5 us
    pallas_call x1, Pallas kernels: 56.7 us -> 55.5 us  [shards(): pl.pallas_call(functools.partial(layer_kernel, scale), out_shape=results,...]
where the time goes in v3:
time: 57.3 us; the launch traced here: 57.2 us
  Pallas kernels  56.5 us (99%)
  between operations  0.64 us (1%)
    pallas_call x1, Pallas kernels, shards(): pl.pallas_call(functools.partial(layer_kernel, scale), out_shape=results,...  55.5 us

profile of v3, /device:TPU:1, one launch (start us, length us, event | category | flops | bytes accessed | tf_op | source)
XLA Modules:
  0.0 57.2 jit_solution(14720942904909702893)
XLA Ops:
  0.6 55.5 %layer.1 = (bf16[1536,128]{1,0:T(8,128)(2,1)S(1)}, bf16[1536,128]{1,0:T(8,128)(2,1)S(1)}, f32[128,128]{1,0:T(8,128)S(1)}, f32[256,128]{1,0:T(8,128)S(1)}, f32[1,...) custom-call(bf16[1536,128]{1,0:T(8,128)(2,1)} %x_hbm.1, ...), custom_call_target="tpu_custom_call" | custom-call | tf_op jit(solution)/shard_map/layer/pallas_call | solution.py:388
  56.2 1.0 %finish.1 = (bf16[1536,128]{1,0:T(8,128)(2,1)}, bf16[1536,128]{1,0:T(8,128)(2,1)}, f32[128,128]{1,0:T(8,128)}, f32[256,128]{1,0:T(8,128)}, f32[1,128]{1,0:T(1,12...) custom-call(bf16[1536,128]{1,0:T(8,128)(2,1)S(1)} %get-tuple-element.24.refs_0_, ...), custom_call_target="tpu_custom_call" | custom-call | tf_op jit(solution)/shard_map/finish/pallas_call | solution.py:420
